TPU v7x, 512 devices: a whole 4x4x16 slice. The times are simulated.
512 devices in a mesh: seq: 128 (over z, y, x_hi), branch: 4 (over x_lo, core).
Axes of the slice: x: 4 (x_hi: 2, x_lo: 2; x = x_hi * 2 + x_lo), y: 4, z: 16, core: 2. Of those that a mesh axis runs over, the one named last changes fastest.
Arguments:
- q_ctl: bfloat16 [4, 24576, 2048], P('branch', 'seq'), may hold values from -64 to 64
- k_ctl: bfloat16 [4, 24576, 2048], P('branch', 'seq'), may hold values from -64 to 64
- v_ctl: bfloat16 [4, 24576, 2048], P('branch', 'seq'), may hold values from -6 to 6
- positions: int32 [24576], P('seq'), may hold values from 0 to 12287
- branch_ids: int32 [4], P('branch'), may hold values from 0 to 63
- cond_scale: float32 [64], replicated, may hold values from 0.25 to 2
- out_weight: bfloat16 [2048, 3072], P('branch', 'seq'), may hold values from -0.125 to 0.125
- frozen: bfloat16 [24576, 3072], P(('seq', 'branch')), may hold values from -2.390625 to 2.390625
- norm_gain: float32 [3072], replicated, may hold values from 0.5 to 1.5
- cotangent: bfloat16 [24576, 3072], P('seq'), may hold values from -6 to 6
Outputs:
- normed: bfloat16 [24576, 3072], P(('seq', 'branch'))
- grad_attn: bfloat16 [4, 24576, 2048], P('branch', 'seq')
All inputs are finite; a program needn't handle non-finite values.
Results may differ from a plain program's by a relative error of at most 0.014.
Values may be sent and summed in bfloat16 or wider, within the bound.
No kernel may reach another device: no remote copies, remote signals or barrier semaphores. Data moves between devices by JAX's collectives and lax.ppermute only.
A program may use at most 64 MiB of HBM per device.

v0:
```python
import math
import jax
import jax.numpy as jnp
from jax import lax
from jax.sharding import PartitionSpec as P

HEADS = 16
HEAD_DIM = 128
EPS = 1e-06


def from_partner(shard, axis, distance):
    return lax.ppermute(shard, axis, [(i, i ^ 1 << distance) for i in range(lax.axis_size(axis))])


def rope_tables(positions, head_dim):
    exponents = jnp.arange(head_dim // 2, dtype=jnp.float32) * (2.0 / head_dim)
    frequencies = 10000.0 ** (-exponents)
    angles = positions.astype(jnp.float32)[..., None] * frequencies
    return (jnp.cos(angles), jnp.sin(angles))


def rotate(values_in, cosines, sines):
    half_dim = values_in.shape[-1] // 2
    front_half = values_in[..., :half_dim]
    back_half = values_in[..., half_dim:]
    return jnp.concatenate(
        [front_half * cosines - back_half * sines, back_half * cosines + front_half * sines],
        axis=-1,
    )


def normalize(hidden, norm_gain):
    inverse = lax.rsqrt(jnp.mean(hidden * hidden, axis=-1, keepdims=True) + EPS)
    return (hidden * inverse * norm_gain).astype(jnp.bfloat16)


def norm_grad(hidden, norm_gain, cotangent):
    inverse = lax.rsqrt(jnp.mean(hidden * hidden, axis=-1, keepdims=True) + EPS)
    upstream = cotangent.astype(jnp.float32) * norm_gain
    inner_mean = jnp.mean(upstream * hidden, axis=-1, keepdims=True)
    return (inverse * upstream - hidden * (inverse * inverse * inverse) * inner_mean).astype(
        jnp.bfloat16
    )


def attend_head(packed):
    query_rows, key_rows, value_rows = packed
    clip_len = query_rows.shape[0]
    block_rows = min(512, clip_len)
    factor = 1.0 / math.sqrt(query_rows.shape[-1])

    def one_block(query_block):
        scores = jnp.dot(query_block, key_rows.T, preferred_element_type=jnp.float32) * factor
        row_max = jnp.max(scores, axis=-1, keepdims=True)
        weights = jnp.exp(scores - row_max)
        row_total = jnp.sum(weights, axis=-1, keepdims=True)
        weights_low = (weights / row_total).astype(jnp.bfloat16)
        return jnp.dot(weights_low, value_rows, preferred_element_type=jnp.float32).astype(
            jnp.bfloat16
        )

    blocks = query_rows.reshape(clip_len // block_rows, block_rows, query_rows.shape[-1])
    return lax.map(one_block, blocks).reshape(clip_len, query_rows.shape[-1])


def regroup(buffer, group_bits, seq_index, forward):
    full_shape = buffer.shape
    split = buffer.reshape(full_shape[:1] + (2,) * group_bits + full_shape[2:])
    for bit in range(group_bits):
        axis_here = group_bits - bit
        mine = jnp.bitwise_and(jnp.right_shift(seq_index, bit), 1)
        other = 1 - mine
        outgoing = lax.dynamic_index_in_dim(split, other, axis_here, keepdims=True)
        if forward:
            incoming = from_partner(outgoing, "seq", bit)
        else:
            incoming = from_partner(outgoing, "seq", bit)
        split = lax.dynamic_update_index_in_dim(split, incoming, other, axis_here)
    return split.reshape(full_shape)


def on_device(
    q_ctl, k_ctl, v_ctl, positions, branch_ids, cond_scale, out_weight, frozen, norm_gain, cotangent
):
    branch_index = lax.axis_index("branch")
    quarters = lax.axis_size("branch")
    seq_index = lax.axis_index("seq")
    seq_devices = lax.axis_size("seq")
    group = min(HEADS, seq_devices)
    group_bits = group.bit_length() - 1
    local_len = q_ctl.shape[1]
    feature_width = q_ctl.shape[2]
    head_dim = HEAD_DIM
    head_count = feature_width // head_dim
    heads_here = head_count // group
    clip_len = group * local_len
    quarter_len = local_len // quarters
    model_width = cotangent.shape[1]
    cosines, sines = rope_tables(positions, head_dim)
    cosines = cosines[:, None, :]
    sines = sines[:, None, :]

    def heads_first(source, rotated):
        split_heads = source[0].reshape(local_len, head_count, head_dim)
        if rotated:
            split_heads = rotate(split_heads.astype(jnp.float32), cosines, sines).astype(
                jnp.bfloat16
            )
        split_heads = split_heads.reshape(local_len, group, heads_here, head_dim)
        return jnp.transpose(split_heads, (1, 0, 2, 3))

    stacked = jnp.stack(
        [heads_first(q_ctl, True), heads_first(k_ctl, True), heads_first(v_ctl, False)]
    )
    arrived = regroup(stacked, group_bits, seq_index, True)

    def per_head(member):
        return jnp.transpose(member, (2, 0, 1, 3)).reshape(heads_here, clip_len, head_dim)

    attended_heads = lax.map(
        attend_head, (per_head(arrived[0]), per_head(arrived[1]), per_head(arrived[2]))
    )
    going_back = jnp.transpose(
        attended_heads.reshape(heads_here, group, local_len, head_dim), (1, 2, 0, 3)
    )[None]
    returned = regroup(going_back, group_bits, seq_index, False)[0]
    attended = jnp.transpose(returned, (1, 0, 2, 3)).reshape(local_len, feature_width)
    branch_scale = jnp.sum(
        jnp.where(jnp.arange(cond_scale.shape[0]) == branch_ids[0], cond_scale, 0.0)
    )
    weight_rows = lax.all_gather(out_weight, "seq", axis=1, tiled=True)
    mixed = lax.psum_scatter(
        (branch_scale * attended.astype(jnp.float32)).astype(jnp.bfloat16),
        "branch",
        scatter_dimension=1,
        tiled=True,
    ).astype(jnp.float32)
    mixed_high = mixed.astype(jnp.bfloat16)
    mixed_rest = (mixed - mixed_high.astype(jnp.float32)).astype(jnp.bfloat16)
    partial_stream = jnp.dot(mixed_high, weight_rows, preferred_element_type=jnp.float32)
    partial_stream = partial_stream + jnp.dot(
        mixed_rest, weight_rows, preferred_element_type=jnp.float32
    )
    owner = (jnp.arange(quarters) == branch_index).astype(jnp.float32)[:, None, None]
    term = (
        partial_stream.reshape(quarters, quarter_len, model_width)
        + owner * frozen.astype(jnp.float32)[None]
    )
    hidden = (
        lax.psum(term.astype(jnp.bfloat16), "branch")
        .astype(jnp.float32)
        .reshape(local_len, model_width)
    )
    hidden_share = lax.dynamic_slice_in_dim(hidden, branch_index * quarter_len, quarter_len, 0)
    normed = normalize(hidden_share, norm_gain)
    grad_hidden = norm_grad(hidden, norm_gain, cotangent)
    cot_block = jnp.einsum(
        "td,hd->th", grad_hidden, weight_rows, preferred_element_type=jnp.float32
    ).astype(jnp.bfloat16)
    cot_attn = lax.all_gather(cot_block, "branch", axis=1, tiled=True)
    grad_attn = (branch_scale * cot_attn.astype(jnp.float32)).astype(jnp.bfloat16)
    return (normed, grad_attn.reshape(1, local_len, feature_width))


def solution(mesh):
    return jax.shard_map(
        on_device,
        mesh=mesh,
        in_specs=(
            P("branch", "seq", None),
            P("branch", "seq", None),
            P("branch", "seq", None),
            P("seq"),
            P("branch"),
            P(),
            P("branch", "seq"),
            P(("seq", "branch"), None),
            P(),
            P("seq", None),
        ),
        out_specs=(P(("seq", "branch"), None), P("branch", "seq", None)),
        check_vma=False,
    )
```

profile of v0, /device:TPU:1, one launch (start us, length us, event | category | flops | bytes accessed | tf_op | source)
XLA Modules:
  0.0 424.5 jit_solution(8821610244191821590)
XLA Ops:
  8.7 1.4 convert_bitcast_fusion.1
  15.9 1.6 pad_maximum_fusion
  18.6 5.4 %collective-permute-start = (bf16[3,2,2,2,1,192,1,128]{7,5,4,3,2,1,6,0:T(8,128)(2,1)}, bf16[3,2,2,2,1,192,1,128]{7,5,4,3,2,1,6,0:T(8,128)(2,1)S(1)}, u32[]{:S(2)}, u32[]{:S(2)}) collective-permute-start(bf16[3,2,2,2,1,192,1,128]{7,5,4,3,2,1,6,0:T(8,128)(2,1)} %constant_dynamic-slice_fusion.7), channel_id=1, source_target_pairs={{0,4},{4,0},{8,12},{12,8},{16,20},{20,16},{24,28},{28,24},{32,36},... | collective-permute-start | bytes 3538952 | tf_op jit(solution)/shard_map/ppermute | solution.py:13
  24.1 22.6 %collective-permute-done = bf16[3,2,2,2,1,192,1,128]{7,5,4,3,2,1,6,0:T(8,128)(2,1)S(1)} collective-permute-done((bf16[3,2,2,2,1,192,1,128]{7,5,4,3,2,1,6,0:T(8,128)(2,1)}, bf16[3,2,2,2,1,192,1,128]{7,5,4,3,2,1,6,0:T(8,128)(2,1)S(1)}, u32[]{:S(2)}, u32[]{:S(2)}) %collective-permute-start) | collective-permute-done | bytes 1179680 | tf_op jit(solution)/shard_map/ppermute | solution.py:13
  47.9 6.5 %collective-permute-start.1 = (bf16[3,2,2,1,2,192,1,128]{7,5,4,3,2,1,6,0:T(8,128)(2,1)}, bf16[3,2,2,1,2,192,1,128]{7,5,4,3,2,1,6,0:T(8,128)(2,1)S(1)}, u32[]{:S(2)}, u32[]{:S(2)}) collective-permute-start(bf16[3,2,2,1,2,192,1,128]{7,5,4,3,2,1,6,0:T(8,128)(2,1)} %constant_dynamic-slice_fusion.6), channel_id=1, source_target_pairs={{0,8},{4,12},{8,0},{12,4},{16,24},{20,28},{24,16},{28,20},{32,40},... | collective-permute-start | bytes 3538952 | tf_op jit(solution)/shard_map/ppermute | solution.py:13
  54.4 24.8 %collective-permute-done.1 = bf16[3,2,2,1,2,192,1,128]{7,5,4,3,2,1,6,0:T(8,128)(2,1)S(1)} collective-permute-done((bf16[3,2,2,1,2,192,1,128]{7,5,4,3,2,1,6,0:T(8,128)(2,1)}, bf16[3,2,2,1,2,192,1,128]{7,5,4,3,2,1,6,0:T(8,128)(2,1)S(1)}, u32[]{:S(2)}, u32[]{:S(2)}) %collective-permute-start.1) | collective-permute-done | bytes 1179680 | tf_op jit(solution)/shard_map/ppermute | solution.py:13
  80.5 4.9 %collective-permute-start.2 = (bf16[3,2,1,2,2,192,1,128]{7,5,4,3,2,1,6,0:T(8,128)(2,1)}, bf16[3,2,1,2,2,192,1,128]{7,5,4,3,2,1,6,0:T(8,128)(2,1)S(1)}, u32[]{:S(2)}, u32[]{:S(2)}) collective-permute-start(bf16[3,2,1,2,2,192,1,128]{7,5,4,3,2,1,6,0:T(8,128)(2,1)} %constant_dynamic-slice_fusion.5), channel_id=1, source_target_pairs={{0,16},{4,20},{8,24},{12,28},{16,0},{20,4},{24,8},{28,12},{32,48},... | collective-permute-start | bytes 3538952 | tf_op jit(solution)/shard_map/ppermute | solution.py:13
  85.4 24.0 %collective-permute-done.2 = bf16[3,2,1,2,2,192,1,128]{7,5,4,3,2,1,6,0:T(8,128)(2,1)S(1)} collective-permute-done((bf16[3,2,1,2,2,192,1,128]{7,5,4,3,2,1,6,0:T(8,128)(2,1)}, bf16[3,2,1,2,2,192,1,128]{7,5,4,3,2,1,6,0:T(8,128)(2,1)S(1)}, u32[]{:S(2)}, u32[]{:S(2)}) %collective-permute-start.2) | collective-permute-done | bytes 1179680 | tf_op jit(solution)/shard_map/ppermute | solution.py:13
  110.8 3.5 collective-permute-start.3
  114.3 23.2 %collective-permute-done.3 = bf16[3,1,2,2,2,192,1,128]{7,5,4,3,2,1,6,0:T(8,128)(2,1)S(1)} collective-permute-done((bf16[3,1,2,2,2,192,1,128]{7,5,4,3,2,1,6,0:T(8,128)(2,1)}, bf16[3,1,2,2,2,192,1,128]{7,5,4,3,2,1,6,0:T(8,128)(2,1)S(1)}, u32[]{:S(2)}, u32[]{:S(2)}) %collective-permute-start.3) | collective-permute-done | bytes 1179680 | tf_op jit(solution)/shard_map/ppermute | solution.py:13
  137.7 1.4 fusion.22
  139.0 31.2 %while.17 = (s32[]{:T(128)}, bf16[6,512,128]{2,1,0:T(8,128)(2,1)}, bf16[6,512,128]{2,1,0:T(8,128)(2,1)}, bf16[3072,128]{1,0:T(8,128)(2,1)S(1)}, bf16[3072,128]{1,0:T(8,128)(2,1)}, /*index=5*/s32[]{:T(128)}) while((s32[]{:T(128)}, bf16[6,512,128]{2,1,0:T(8,128)(2,1)}, bf16[6,512,128]{2,1,0:T(8,128)(2,1)}, bf16[3072,128]{1,0:T(8,128)(2,1)S(1)}, ...), condition=%wide.region_4.5_spmd, body=%wide.region_1.4_spmd.sunk | while | flops 819526656 | bytes 23866464 | solution.py:64
  139.0 2.0 multiply_reduce_fusion.5
  141.0 1.2 fusion.36
  142.2 2.1 fusion.37
  144.2 2.0 multiply_reduce_fusion.5
  146.2 1.2 fusion.36
  147.4 2.1 fusion.37
  149.4 2.0 multiply_reduce_fusion.5
  151.4 1.2 fusion.36
  152.6 2.1 fusion.37
  154.6 2.0 multiply_reduce_fusion.5
  156.6 1.2 fusion.36
  157.8 2.1 fusion.37
  159.8 2.0 multiply_reduce_fusion.5
  161.8 1.2 fusion.36
  163.0 2.1 fusion.37
  165.0 2.0 multiply_reduce_fusion.5
  167.0 1.2 fusion.36
  168.2 2.1 fusion.37
  171.3 4.6 %collective-permute-start.4 = (bf16[1,2,2,2,1,192,1,128]{7,5,4,3,2,1,6,0:T(8,128)(2,1)S(1)}, bf16[1,2,2,2,1,192,1,128]{7,5,4,3,2,1,6,0:T(8,128)(2,1)S(1)}, u32[]{:S(2)}, u32[]{:S(2)}) collective-permute-start(bf16[1,2,2,2,1,192,1,128]{7,5,4,3,2,1,6,0:T(8,128)(2,1)S(1)} %constant_dynamic-slice_fusion.3), channel_id=1, source_target_pairs={{0,4},{4,0},{8,12},{12,8},{16,20},{20,16},{24,28},{28,24},{32,36},... | collective-permute-start | bytes 1179656 | tf_op jit(solution)/shard_map/ppermute | solution.py:13
  175.9 5.4 %collective-permute-done.4 = bf16[1,2,2,2,1,192,1,128]{7,5,4,3,2,1,6,0:T(8,128)(2,1)S(1)} collective-permute-done((bf16[1,2,2,2,1,192,1,128]{7,5,4,3,2,1,6,0:T(8,128)(2,1)S(1)}, bf16[1,2,2,2,1,192,1,128]{7,5,4,3,2,1,6,0:T(8,128)(2,1)S(1)}, u32[]{:S(2)}, u32[]{:S(2)}) %collective-permute-start.4) | collective-permute-done | bytes 393248 | tf_op jit(solution)/shard_map/ppermute | solution.py:13
  183.2 3.2 collective-permute-start.5
  186.3 5.7 %collective-permute-done.5 = bf16[1,2,2,1,2,192,1,128]{7,5,4,3,2,1,6,0:T(8,128)(2,1)S(1)} collective-permute-done((bf16[1,2,2,1,2,192,1,128]{7,5,4,3,2,1,6,0:T(8,128)(2,1)S(1)}, bf16[1,2,2,1,2,192,1,128]{7,5,4,3,2,1,6,0:T(8,128)(2,1)S(1)}, u32[]{:S(2)}, u32[]{:S(2)}) %collective-permute-start.5) | collective-permute-done | bytes 393248 | tf_op jit(solution)/shard_map/ppermute | solution.py:13
  193.9 4.8 %collective-permute-start.6 = (bf16[1,2,1,2,2,192,1,128]{7,5,4,3,2,1,6,0:T(8,128)(2,1)S(1)}, bf16[1,2,1,2,2,192,1,128]{7,5,4,3,2,1,6,0:T(8,128)(2,1)S(1)}, u32[]{:S(2)}, u32[]{:S(2)}) collective-permute-start(bf16[1,2,1,2,2,192,1,128]{7,5,4,3,2,1,6,0:T(8,128)(2,1)S(1)} %constant_dynamic-slice_fusion.1), channel_id=1, source_target_pairs={{0,16},{4,20},{8,24},{12,28},{16,0},{20,4},{24,8},{28,12},{32,48},... | collective-permute-start | bytes 1179656 | tf_op jit(solution)/shard_map/ppermute | solution.py:13
  198.7 5.2 %collective-permute-done.6 = bf16[1,2,1,2,2,192,1,128]{7,5,4,3,2,1,6,0:T(8,128)(2,1)S(1)} collective-permute-done((bf16[1,2,1,2,2,192,1,128]{7,5,4,3,2,1,6,0:T(8,128)(2,1)S(1)}, bf16[1,2,1,2,2,192,1,128]{7,5,4,3,2,1,6,0:T(8,128)(2,1)S(1)}, u32[]{:S(2)}, u32[]{:S(2)}) %collective-permute-start.6) | collective-permute-done | bytes 393248 | tf_op jit(solution)/shard_map/ppermute | solution.py:13
  205.8 3.5 collective-permute-start.7
  210.6 4.3 %collective-permute-done.7 = bf16[1,1,2,2,2,192,1,128]{7,5,4,3,2,1,6,0:T(8,128)(2,1)S(1)} collective-permute-done((bf16[1,1,2,2,2,192,1,128]{7,5,4,3,2,1,6,0:T(8,128)(2,1)S(1)}, bf16[1,1,2,2,2,192,1,128]{7,5,4,3,2,1,6,0:T(8,128)(2,1)S(1)}, u32[]{:S(2)}, u32[]{:S(2)}) %collective-permute-start.7) | collective-permute-done | bytes 393248 | tf_op jit(solution)/shard_map/ppermute | solution.py:13
  215.6 2.0 multiply_convert_fusion.1
  220.4 109.9 %all-gather.2.cloned.1.call-done = bf16[512,3072]{0,1:T(8,128)(2,1)} async-done(((bf16[512,24]{0,1:T(8,128)(2,1)}), bf16[512,3072]{0,1:T(8,128)(2,1)}) %all-gather.2.cloned.1.call-update) | async-done | bytes 3145744 | tf_op jit(solution)/shard_map/all_gather | solution.py:132
  330.4 3.3 fusion.23
  333.7 1.2 convolution_add_fusion
  334.9 1.3 add_convert_fusion
  336.3 62.4 %all-reduce.2.cloned.1.call-done = bf16[4,48,3072]{2,1,0:T(8,128)(2,1)} async-done(((bf16[4,48,3072]{2,1,0:T(8,128)(2,1)}), bf16[4,48,3072]{2,1,0:T(8,128)(2,1)}) %all-reduce.2.cloned.1.call-update) | async-done | bytes 1179664 | tf_op jit(solution)/shard_map/psum | solution.py:151
  398.7 3.5 multiply_reduce_fusion.1
  402.7 2.8 fusion.15
  405.5 8.8 %all_gather.7 = bf16[192,2048]{1,0:T(8,128)(2,1)S(1)} all-gather(bf16[192,512]{1,0:T(8,128)(2,1)S(1)} %fusion.15), channel_id=1, replica_groups=mesh['seq'=128,'branch'=4] {'branch'}, dimensions={1}, use_global_device_ids=true | all-gather | bytes 983040 | tf_op jit(solution)/shard_map/all_gather | solution.py:161
  414.4 1.7 fusion.20
  (81 shorter events, 24.0 us)
Async XLA Ops:
  8.0 322.4 %all-gather.2.cloned.1.call-start = ((), (), s32[]{:S(2)}) async-start(), calls=%async_computation.2 | async-start | bytes 3170304 | tf_op jit(solution)/shard_map/all_gather | solution.py:132
  8.7 1.7 copy-start.7
  13.3 1.3 copy-start.6
  18.6 28.0 %collective-permute-start = (bf16[3,2,2,2,1,192,1,128]{7,5,4,3,2,1,6,0:T(8,128)(2,1)}, bf16[3,2,2,2,1,192,1,128]{7,5,4,3,2,1,6,0:T(8,128)(2,1)S(1)}, u32[]{:S(2)}, u32[]{:S(2)}) collective-permute-start(bf16[3,2,2,2,1,192,1,128]{7,5,4,3,2,1,6,0:T(8,128)(2,1)} %constant_dynamic-slice_fusion.7), channel_id=1, source_target_pairs={{0,4},{4,0},{8,12},{12,8},{16,20},{20,16},{24,28},{28,24},{32,36},... | collective-permute-start | bytes 3538952 | tf_op jit(solution)/shard_map/ppermute | solution.py:13
  47.9 31.3 %collective-permute-start.1 = (bf16[3,2,2,1,2,192,1,128]{7,5,4,3,2,1,6,0:T(8,128)(2,1)}, bf16[3,2,2,1,2,192,1,128]{7,5,4,3,2,1,6,0:T(8,128)(2,1)S(1)}, u32[]{:S(2)}, u32[]{:S(2)}) collective-permute-start(bf16[3,2,2,1,2,192,1,128]{7,5,4,3,2,1,6,0:T(8,128)(2,1)} %constant_dynamic-slice_fusion.6), channel_id=1, source_target_pairs={{0,8},{4,12},{8,0},{12,4},{16,24},{20,28},{24,16},{28,20},{32,40},... | collective-permute-start | bytes 3538952 | tf_op jit(solution)/shard_map/ppermute | solution.py:13
  80.5 28.9 %collective-permute-start.2 = (bf16[3,2,1,2,2,192,1,128]{7,5,4,3,2,1,6,0:T(8,128)(2,1)}, bf16[3,2,1,2,2,192,1,128]{7,5,4,3,2,1,6,0:T(8,128)(2,1)S(1)}, u32[]{:S(2)}, u32[]{:S(2)}) collective-permute-start(bf16[3,2,1,2,2,192,1,128]{7,5,4,3,2,1,6,0:T(8,128)(2,1)} %constant_dynamic-slice_fusion.5), channel_id=1, source_target_pairs={{0,16},{4,20},{8,24},{12,28},{16,0},{20,4},{24,8},{28,12},{32,48},... | collective-permute-start | bytes 3538952 | tf_op jit(solution)/shard_map/ppermute | solution.py:13
  110.8 26.7 %collective-permute-start.3 = (bf16[3,1,2,2,2,192,1,128]{7,5,4,3,2,1,6,0:T(8,128)(2,1)}, bf16[3,1,2,2,2,192,1,128]{7,5,4,3,2,1,6,0:T(8,128)(2,1)S(1)}, u32[]{:S(2)}, u32[]{:S(2)}) collective-permute-start(bf16[3,1,2,2,2,192,1,128]{7,5,4,3,2,1,6,0:T(8,128)(2,1)} %constant_dynamic-slice_fusion.4), channel_id=1, source_target_pairs={{0,32},{4,36},{8,40},{12,44},{16,48},{20,52},{24,56},{28,60},{32,0... | collective-permute-start | bytes 3538952 | tf_op jit(solution)/shard_map/ppermute | solution.py:13
  114.3 216.1 %reduce-scatter.2.cloned.1.call-start = ((), (), s32[]{:S(2)}) async-start(), calls=%async_computation.1 | async-start | bytes 983040 | tf_op jit(solution)/shard_map/reduce_scatter | solution.py:133
  141.0 1.2 copy-start.4
  146.2 1.2 copy-start.4
  151.4 1.2 copy-start.4
  156.6 1.2 copy-start.4
  161.8 1.2 copy-start.4
  167.0 1.2 copy-start.4
  171.3 38.6 %copy-start.10 = (f32[64]{0:T(128)S(1)}, f32[64]{0:T(128)}, u32[]{:S(2)}) copy-start(f32[64]{0:T(128)} %param.17) | copy-start | bytes 772
  171.3 10.0 %collective-permute-start.4 = (bf16[1,2,2,2,1,192,1,128]{7,5,4,3,2,1,6,0:T(8,128)(2,1)S(1)}, bf16[1,2,2,2,1,192,1,128]{7,5,4,3,2,1,6,0:T(8,128)(2,1)S(1)}, u32[]{:S(2)}, u32[]{:S(2)}) collective-permute-start(bf16[1,2,2,2,1,192,1,128]{7,5,4,3,2,1,6,0:T(8,128)(2,1)S(1)} %constant_dynamic-slice_fusion.3), channel_id=1, source_target_pairs={{0,4},{4,0},{8,12},{12,8},{16,20},{20,16},{24,28},{28,24},{32,36},... | collective-permute-start | bytes 1179656 | tf_op jit(solution)/shard_map/ppermute | solution.py:13
  183.2 8.9 %collective-permute-start.5 = (bf16[1,2,2,1,2,192,1,128]{7,5,4,3,2,1,6,0:T(8,128)(2,1)S(1)}, bf16[1,2,2,1,2,192,1,128]{7,5,4,3,2,1,6,0:T(8,128)(2,1)S(1)}, u32[]{:S(2)}, u32[]{:S(2)}) collective-permute-start(bf16[1,2,2,1,2,192,1,128]{7,5,4,3,2,1,6,0:T(8,128)(2,1)S(1)} %constant_dynamic-slice_fusion.2), channel_id=1, source_target_pairs={{0,8},{4,12},{8,0},{12,4},{16,24},{20,28},{24,16},{28,20},{32,40},... | collective-permute-start | bytes 1179656 | tf_op jit(solution)/shard_map/ppermute | solution.py:13
  193.9 10.0 %collective-permute-start.6 = (bf16[1,2,1,2,2,192,1,128]{7,5,4,3,2,1,6,0:T(8,128)(2,1)S(1)}, bf16[1,2,1,2,2,192,1,128]{7,5,4,3,2,1,6,0:T(8,128)(2,1)S(1)}, u32[]{:S(2)}, u32[]{:S(2)}) collective-permute-start(bf16[1,2,1,2,2,192,1,128]{7,5,4,3,2,1,6,0:T(8,128)(2,1)S(1)} %constant_dynamic-slice_fusion.1), channel_id=1, source_target_pairs={{0,16},{4,20},{8,24},{12,28},{16,0},{20,4},{24,8},{28,12},{32,48},... | collective-permute-start | bytes 1179656 | tf_op jit(solution)/shard_map/ppermute | solution.py:13
  205.8 9.1 %collective-permute-start.7 = (bf16[1,1,2,2,2,192,1,128]{7,5,4,3,2,1,6,0:T(8,128)(2,1)S(1)}, bf16[1,1,2,2,2,192,1,128]{7,5,4,3,2,1,6,0:T(8,128)(2,1)S(1)}, u32[]{:S(2)}, u32[]{:S(2)}) collective-permute-start(bf16[1,1,2,2,2,192,1,128]{7,5,4,3,2,1,6,0:T(8,128)(2,1)S(1)} %constant_dynamic-slice_fusion), channel_id=1, source_target_pairs={{0,32},{4,36},{8,40},{12,44},{16,48},{20,52},{24,56},{28,60},{32,0... | collective-permute-start | bytes 1179656 | tf_op jit(solution)/shard_map/ppermute | solution.py:13
  217.6 2.0 copy-start.8
  219.5 179.2 %all-reduce.2.cloned.1.call-start = ((), (), s32[]{:S(2)}) async-start(), calls=%async_computation.3 | async-start | bytes 2359296 | tf_op jit(solution)/shard_map/psum | solution.py:151
  330.4 3.3 copy-start
  330.4 3.3 copy-start.5
  333.7 1.2 copy-start.3
  334.9 63.8 %copy-start.9 = (f32[3072]{0:T(1024)S(1)}, f32[3072]{0:T(1024)}, u32[]{:S(2)}) copy-start(f32[3072]{0:T(1024)} %param.20) | copy-start | bytes 36868
  398.7 3.5 copy-start.2
  405.5 10.5 %copy-start.1 = (f32[192,3072]{1,0:T(8,128)S(1)}, f32[192,3072]{1,0:T(8,128)}, u32[]{:S(2)}) copy-start(f32[192,3072]{1,0:T(8,128)} %get-tuple-element.56) | copy-start | bytes 7077892
Sparse Core Ops, SparseCore 0:
  114.4 215.9 all-gather.1
Sparse Core Ops, SparseCore 1:
  219.6 39.7 reduce-scatter.1
  336.4 62.3 all-reduce.1
where the time goes:
time: 425 us; the launch traced here: 424 us
  waiting for transfers between devices  288 us (68%)
  starting transfers between devices  36.4 us (9%)
  matrix products  31.5 us (7%)
  other arithmetic  24.5 us (6%)
  local copies, waits for them, and re-layouts  19.1 us (4%)
  between operations  16.5 us (4%)
  blocking collectives  8.84 us (2%)
    ppermute x8, waiting for transfers between devices, from_partner(): lax.ppermute(shard, axis, [(i, i ^ 1 << distance) for i in range(lax.axis...  115 us
    all_gather x1, waiting for transfers between devices, on_device(): weight_rows = lax.all_gather(out_weight, 'seq', axis=1, tiled=True)  110 us
    psum x1, waiting for transfers between devices, on_device(): lax.psum(term.astype(jnp.bfloat16), 'branch').astype(jnp.float32)  62.4 us
    ppermute x8, starting transfers between devices, from_partner(): lax.ppermute(shard, axis, [(i, i ^ 1 << distance) for i in range(lax.axis...  36.3 us
    dot_general x6, matrix products, one_block(): jnp.dot(weights_low, value_rows, preferred_element_type=jnp.float32)  12.4 us
    dot_general x6, matrix products, one_block(): jnp.dot(query_block, key_rows.T, preferred_element_type=jnp.float32)  11.8 us
    all_gather x1, blocking collectives, on_device(): cot_attn = lax.all_gather(cot_block, 'branch', axis=1, tiled=True)  8.84 us
    dynamic_slice x8, local copies, waits for them, and re-layouts, regroup(): outgoing = lax.dynamic_index_in_dim(split, other, axis_here, keepdims=True)  8.65 us
  transfers between devices with their start and end apart: 11, of which 10 were waited for; matrix products, arithmetic and copies ran while one was open for 11% of the time, Pallas kernels for 0%

commit v1 on v0

--- a/solution.py
+++ b/solution.py
@@ -148,7 +148,7 @@
         + owner * frozen.astype(jnp.float32)[None]
     )
     hidden = (
-        lax.psum(term.astype(jnp.bfloat16), "branch")
+        jnp.sum(lax.all_gather(term.astype(jnp.bfloat16), "branch"), axis=0)
         .astype(jnp.float32)
         .reshape(local_len, model_width)
     )

time: 425 us -> 432 us (1.016)
  other arithmetic: 24.5 us -> 30.5 us
    all_gather x0 -> x1, waiting for transfers between devices: none -> 63 us  [on_device(): lax.all_gather(term.astype(jnp.bfloat16), 'branch')]
    psum x1 -> x0, waiting for transfers between devices: 62.4 us -> none  [on_device(): lax.psum(term.astype(jnp.bfloat16), 'branch').astype(jnp.float32)]
    reduce_sum x0 -> x1, other arithmetic: none -> 4.62 us  [on_device(): jnp.sum(lax.all_gather(term.astype(jnp.bfloat16), 'branch'), axis=0)]
where the time goes in v1:
time: 432 us; the launch traced here: 431 us
  waiting for transfers between devices  288 us (67%)
  starting transfers between devices  36.4 us (8%)
  matrix products  31.5 us (7%)
  other arithmetic  30.5 us (7%)
  local copies, waits for them, and re-layouts  19.1 us (4%)
  between operations  16.5 us (4%)
  blocking collectives  8.59 us (2%)
    ppermute x8, waiting for transfers between devices, from_partner(): lax.ppermute(shard, axis, [(i, i ^ 1 << distance) for i in range(lax.axis...  115 us
    all_gather x1, waiting for transfers between devices, on_device(): weight_rows = lax.all_gather(out_weight, 'seq', axis=1, tiled=True)  110 us
    all_gather x1, waiting for transfers between devices, on_device(): lax.all_gather(term.astype(jnp.bfloat16), 'branch')  63 us
    ppermute x8, starting transfers between devices, from_partner(): lax.ppermute(shard, axis, [(i, i ^ 1 << distance) for i in range(lax.axis...  36.2 us
    dot_general x6, matrix products, one_block(): jnp.dot(weights_low, value_rows, preferred_element_type=jnp.float32)  12.4 us
    dot_general x6, matrix products, one_block(): jnp.dot(query_block, key_rows.T, preferred_element_type=jnp.float32)  11.8 us
    dynamic_slice x8, local copies, waits for them, and re-layouts, regroup(): outgoing = lax.dynamic_index_in_dim(split, other, axis_here, keepdims=True)  8.66 us
  transfers between devices with their start and end apart: 11, of which 10 were waited for; matrix products, arithmetic and copies ran while one was open for 11% of the time, Pallas kernels for 0%

profile of v1, /device:TPU:1, one launch (start us, length us, event | category | flops | bytes accessed | tf_op | source)
XLA Modules:
  0.0 430.7 jit_solution(11873562043466279211)
XLA Ops:
  8.7 1.4 convert_bitcast_fusion.1
  15.8 1.6 pad_maximum_fusion
  18.6 5.4 %collective-permute-start = (bf16[3,2,2,2,1,192,1,128]{7,5,4,3,2,1,6,0:T(8,128)(2,1)}, bf16[3,2,2,2,1,192,1,128]{7,5,4,3,2,1,6,0:T(8,128)(2,1)S(1)}, u32[]{:S(2)}, u32[]{:S(2)}) collective-permute-start(bf16[3,2,2,2,1,192,1,128]{7,5,4,3,2,1,6,0:T(8,128)(2,1)} %constant_dynamic-slice_fusion.7), channel_id=1, source_target_pairs={{0,4},{4,0},{8,12},{12,8},{16,20},{20,16},{24,28},{28,24},{32,36},... | collective-permute-start | bytes 3538952 | tf_op jit(solution)/shard_map/ppermute | solution.py:13
  24.0 22.6 %collective-permute-done = bf16[3,2,2,2,1,192,1,128]{7,5,4,3,2,1,6,0:T(8,128)(2,1)S(1)} collective-permute-done((bf16[3,2,2,2,1,192,1,128]{7,5,4,3,2,1,6,0:T(8,128)(2,1)}, bf16[3,2,2,2,1,192,1,128]{7,5,4,3,2,1,6,0:T(8,128)(2,1)S(1)}, u32[]{:S(2)}, u32[]{:S(2)}) %collective-permute-start) | collective-permute-done | bytes 1179680 | tf_op jit(solution)/shard_map/ppermute | solution.py:13
  47.9 6.5 %collective-permute-start.1 = (bf16[3,2,2,1,2,192,1,128]{7,5,4,3,2,1,6,0:T(8,128)(2,1)}, bf16[3,2,2,1,2,192,1,128]{7,5,4,3,2,1,6,0:T(8,128)(2,1)S(1)}, u32[]{:S(2)}, u32[]{:S(2)}) collective-permute-start(bf16[3,2,2,1,2,192,1,128]{7,5,4,3,2,1,6,0:T(8,128)(2,1)} %constant_dynamic-slice_fusion.6), channel_id=1, source_target_pairs={{0,8},{4,12},{8,0},{12,4},{16,24},{20,28},{24,16},{28,20},{32,40},... | collective-permute-start | bytes 3538952 | tf_op jit(solution)/shard_map/ppermute | solution.py:13
  54.4 24.8 %collective-permute-done.1 = bf16[3,2,2,1,2,192,1,128]{7,5,4,3,2,1,6,0:T(8,128)(2,1)S(1)} collective-permute-done((bf16[3,2,2,1,2,192,1,128]{7,5,4,3,2,1,6,0:T(8,128)(2,1)}, bf16[3,2,2,1,2,192,1,128]{7,5,4,3,2,1,6,0:T(8,128)(2,1)S(1)}, u32[]{:S(2)}, u32[]{:S(2)}) %collective-permute-start.1) | collective-permute-done | bytes 1179680 | tf_op jit(solution)/shard_map/ppermute | solution.py:13
  80.5 4.9 %collective-permute-start.2 = (bf16[3,2,1,2,2,192,1,128]{7,5,4,3,2,1,6,0:T(8,128)(2,1)}, bf16[3,2,1,2,2,192,1,128]{7,5,4,3,2,1,6,0:T(8,128)(2,1)S(1)}, u32[]{:S(2)}, u32[]{:S(2)}) collective-permute-start(bf16[3,2,1,2,2,192,1,128]{7,5,4,3,2,1,6,0:T(8,128)(2,1)} %constant_dynamic-slice_fusion.5), channel_id=1, source_target_pairs={{0,16},{4,20},{8,24},{12,28},{16,0},{20,4},{24,8},{28,12},{32,48},... | collective-permute-start | bytes 3538952 | tf_op jit(solution)/shard_map/ppermute | solution.py:13
  85.4 24.0 %collective-permute-done.2 = bf16[3,2,1,2,2,192,1,128]{7,5,4,3,2,1,6,0:T(8,128)(2,1)S(1)} collective-permute-done((bf16[3,2,1,2,2,192,1,128]{7,5,4,3,2,1,6,0:T(8,128)(2,1)}, bf16[3,2,1,2,2,192,1,128]{7,5,4,3,2,1,6,0:T(8,128)(2,1)S(1)}, u32[]{:S(2)}, u32[]{:S(2)}) %collective-permute-start.2) | collective-permute-done | bytes 1179680 | tf_op jit(solution)/shard_map/ppermute | solution.py:13
  109.6 1.2 constant_dynamic-slice_fusion.4
  110.8 3.5 collective-permute-start.3
  114.3 23.2 %collective-permute-done.3 = bf16[3,1,2,2,2,192,1,128]{7,5,4,3,2,1,6,0:T(8,128)(2,1)S(1)} collective-permute-done((bf16[3,1,2,2,2,192,1,128]{7,5,4,3,2,1,6,0:T(8,128)(2,1)}, bf16[3,1,2,2,2,192,1,128]{7,5,4,3,2,1,6,0:T(8,128)(2,1)S(1)}, u32[]{:S(2)}, u32[]{:S(2)}) %collective-permute-start.3) | collective-permute-done | bytes 1179680 | tf_op jit(solution)/shard_map/ppermute | solution.py:13
  137.7 1.4 fusion.22
  139.0 31.2 %while.17 = (s32[]{:T(128)}, bf16[6,512,128]{2,1,0:T(8,128)(2,1)}, bf16[6,512,128]{2,1,0:T(8,128)(2,1)}, bf16[3072,128]{1,0:T(8,128)(2,1)S(1)}, bf16[3072,128]{1,0:T(8,128)(2,1)}, /*index=5*/s32[]{:T(128)}) while((s32[]{:T(128)}, bf16[6,512,128]{2,1,0:T(8,128)(2,1)}, bf16[6,512,128]{2,1,0:T(8,128)(2,1)}, bf16[3072,128]{1,0:T(8,128)(2,1)S(1)}, ...), condition=%wide.region_4.5_spmd, body=%wide.region_1.4_spmd.sunk | while | flops 819526656 | bytes 23866464 | solution.py:64
  139.0 2.0 multiply_reduce_fusion.5
  141.0 1.2 fusion.36
  142.2 2.1 fusion.37
  144.2 2.0 multiply_reduce_fusion.5
  146.2 1.2 fusion.36
  147.4 2.1 fusion.37
  149.4 2.0 multiply_reduce_fusion.5
  152.6 2.1 fusion.37
  154.6 2.0 multiply_reduce_fusion.5
  157.8 2.1 fusion.37
  159.8 2.0 multiply_reduce_fusion.5
  161.8 1.2 fusion.36
  163.0 2.1 fusion.37
  165.1 2.0 multiply_reduce_fusion.5
  168.2 2.1 fusion.37
  171.3 4.6 %collective-permute-start.4 = (bf16[1,2,2,2,1,192,1,128]{7,5,4,3,2,1,6,0:T(8,128)(2,1)S(1)}, bf16[1,2,2,2,1,192,1,128]{7,5,4,3,2,1,6,0:T(8,128)(2,1)S(1)}, u32[]{:S(2)}, u32[]{:S(2)}) collective-permute-start(bf16[1,2,2,2,1,192,1,128]{7,5,4,3,2,1,6,0:T(8,128)(2,1)S(1)} %constant_dynamic-slice_fusion.3), channel_id=1, source_target_pairs={{0,4},{4,0},{8,12},{12,8},{16,20},{20,16},{24,28},{28,24},{32,36},... | collective-permute-start | bytes 1179656 | tf_op jit(solution)/shard_map/ppermute | solution.py:13
  175.9 5.4 %collective-permute-done.4 = bf16[1,2,2,2,1,192,1,128]{7,5,4,3,2,1,6,0:T(8,128)(2,1)S(1)} collective-permute-done((bf16[1,2,2,2,1,192,1,128]{7,5,4,3,2,1,6,0:T(8,128)(2,1)S(1)}, bf16[1,2,2,2,1,192,1,128]{7,5,4,3,2,1,6,0:T(8,128)(2,1)S(1)}, u32[]{:S(2)}, u32[]{:S(2)}) %collective-permute-start.4) | collective-permute-done | bytes 393248 | tf_op jit(solution)/shard_map/ppermute | solution.py:13
  183.2 3.2 collective-permute-start.5
  186.3 5.7 %collective-permute-done.5 = bf16[1,2,2,1,2,192,1,128]{7,5,4,3,2,1,6,0:T(8,128)(2,1)S(1)} collective-permute-done((bf16[1,2,2,1,2,192,1,128]{7,5,4,3,2,1,6,0:T(8,128)(2,1)S(1)}, bf16[1,2,2,1,2,192,1,128]{7,5,4,3,2,1,6,0:T(8,128)(2,1)S(1)}, u32[]{:S(2)}, u32[]{:S(2)}) %collective-permute-start.5) | collective-permute-done | bytes 393248 | tf_op jit(solution)/shard_map/ppermute | solution.py:13
  193.9 4.8 %collective-permute-start.6 = (bf16[1,2,1,2,2,192,1,128]{7,5,4,3,2,1,6,0:T(8,128)(2,1)S(1)}, bf16[1,2,1,2,2,192,1,128]{7,5,4,3,2,1,6,0:T(8,128)(2,1)S(1)}, u32[]{:S(2)}, u32[]{:S(2)}) collective-permute-start(bf16[1,2,1,2,2,192,1,128]{7,5,4,3,2,1,6,0:T(8,128)(2,1)S(1)} %constant_dynamic-slice_fusion.1), channel_id=1, source_target_pairs={{0,16},{4,20},{8,24},{12,28},{16,0},{20,4},{24,8},{28,12},{32,48},... | collective-permute-start | bytes 1179656 | tf_op jit(solution)/shard_map/ppermute | solution.py:13
  198.7 5.2 %collective-permute-done.6 = bf16[1,2,1,2,2,192,1,128]{7,5,4,3,2,1,6,0:T(8,128)(2,1)S(1)} collective-permute-done((bf16[1,2,1,2,2,192,1,128]{7,5,4,3,2,1,6,0:T(8,128)(2,1)S(1)}, bf16[1,2,1,2,2,192,1,128]{7,5,4,3,2,1,6,0:T(8,128)(2,1)S(1)}, u32[]{:S(2)}, u32[]{:S(2)}) %collective-permute-start.6) | collective-permute-done | bytes 393248 | tf_op jit(solution)/shard_map/ppermute | solution.py:13
  205.8 3.5 collective-permute-start.7
  210.6 4.2 collective-permute-done.7
  215.6 2.0 multiply_convert_fusion.1
  220.5 109.9 %all-gather.3.cloned.1.call-done = bf16[512,3072]{0,1:T(8,128)(2,1)} async-done(((bf16[512,24]{0,1:T(8,128)(2,1)}), bf16[512,3072]{0,1:T(8,128)(2,1)}) %all-gather.3.cloned.1.call-update) | async-done | bytes 3145744 | tf_op jit(solution)/shard_map/all_gather | solution.py:132
  330.4 3.3 fusion.23
  333.8 1.2 convolution_add_fusion
  335.0 1.4 add_convert_fusion
  336.4 63.0 %all-gather.5.cloned.1.call-done = bf16[4,4,48,3072]{3,2,1,0:T(8,128)(2,1)} async-done(((bf16[1,4,48,3072]{3,2,1,0:T(8,128)(2,1)}), bf16[4,4,48,3072]{3,2,1,0:T(8,128)(2,1)}) %all-gather.5.cloned.1.call-update) | async-done | bytes 4718608 | tf_op jit(solution)/shard_map/all_gather | solution.py:151
  399.4 4.6 %reduce_sum.58 = bf16[4,48,3072]{2,1,0:T(8,128)(2,1)} reduce(bf16[4,4,48,3072]{3,2,1,0:T(8,128)(2,1)} %all-gather.5.cloned.1.call-done, bf16[]{:T(256)} %constant.103.clone.1), dimensions={0}, to_apply=%region_6.7 | reduce | flops 1769472 | bytes 5898242 | tf_op jit(solution)/shard_map/reduce_sum | solution.py:151
  404.0 1.6 multiply_reduce_fusion.2
  405.6 3.4 multiply_reduce_fusion.1
  409.1 2.8 fusion.15
  411.9 8.6 %all_gather.12 = bf16[192,2048]{1,0:T(8,128)(2,1)S(1)} all-gather(bf16[192,512]{1,0:T(8,128)(2,1)S(1)} %fusion.15), channel_id=1, replica_groups=mesh['seq'=128,'branch'=4] {'branch'}, dimensions={1}, use_global_device_ids=true | all-gather | bytes 983040 | tf_op jit(solution)/shard_map/all_gather | solution.py:161
  420.5 1.7 fusion.20
  (80 shorter events, 26.0 us)
Async XLA Ops:
  8.0 322.4 %all-gather.3.cloned.1.call-start = ((), (), s32[]{:S(2)}) async-start(), calls=%async_computation.2 | async-start | bytes 3170304 | tf_op jit(solution)/shard_map/all_gather | solution.py:132
  8.7 1.7 copy-start.6
  13.3 1.3 copy-start.5
  18.6 28.0 %collective-permute-start = (bf16[3,2,2,2,1,192,1,128]{7,5,4,3,2,1,6,0:T(8,128)(2,1)}, bf16[3,2,2,2,1,192,1,128]{7,5,4,3,2,1,6,0:T(8,128)(2,1)S(1)}, u32[]{:S(2)}, u32[]{:S(2)}) collective-permute-start(bf16[3,2,2,2,1,192,1,128]{7,5,4,3,2,1,6,0:T(8,128)(2,1)} %constant_dynamic-slice_fusion.7), channel_id=1, source_target_pairs={{0,4},{4,0},{8,12},{12,8},{16,20},{20,16},{24,28},{28,24},{32,36},... | collective-permute-start | bytes 3538952 | tf_op jit(solution)/shard_map/ppermute | solution.py:13
  47.9 31.3 %collective-permute-start.1 = (bf16[3,2,2,1,2,192,1,128]{7,5,4,3,2,1,6,0:T(8,128)(2,1)}, bf16[3,2,2,1,2,192,1,128]{7,5,4,3,2,1,6,0:T(8,128)(2,1)S(1)}, u32[]{:S(2)}, u32[]{:S(2)}) collective-permute-start(bf16[3,2,2,1,2,192,1,128]{7,5,4,3,2,1,6,0:T(8,128)(2,1)} %constant_dynamic-slice_fusion.6), channel_id=1, source_target_pairs={{0,8},{4,12},{8,0},{12,4},{16,24},{20,28},{24,16},{28,20},{32,40},... | collective-permute-start | bytes 3538952 | tf_op jit(solution)/shard_map/ppermute | solution.py:13
  80.5 28.9 %collective-permute-start.2 = (bf16[3,2,1,2,2,192,1,128]{7,5,4,3,2,1,6,0:T(8,128)(2,1)}, bf16[3,2,1,2,2,192,1,128]{7,5,4,3,2,1,6,0:T(8,128)(2,1)S(1)}, u32[]{:S(2)}, u32[]{:S(2)}) collective-permute-start(bf16[3,2,1,2,2,192,1,128]{7,5,4,3,2,1,6,0:T(8,128)(2,1)} %constant_dynamic-slice_fusion.5), channel_id=1, source_target_pairs={{0,16},{4,20},{8,24},{12,28},{16,0},{20,4},{24,8},{28,12},{32,48},... | collective-permute-start | bytes 3538952 | tf_op jit(solution)/shard_map/ppermute | solution.py:13
  110.8 26.7 %collective-permute-start.3 = (bf16[3,1,2,2,2,192,1,128]{7,5,4,3,2,1,6,0:T(8,128)(2,1)}, bf16[3,1,2,2,2,192,1,128]{7,5,4,3,2,1,6,0:T(8,128)(2,1)S(1)}, u32[]{:S(2)}, u32[]{:S(2)}) collective-permute-start(bf16[3,1,2,2,2,192,1,128]{7,5,4,3,2,1,6,0:T(8,128)(2,1)} %constant_dynamic-slice_fusion.4), channel_id=1, source_target_pairs={{0,32},{4,36},{8,40},{12,44},{16,48},{20,52},{24,56},{28,60},{32,0... | collective-permute-start | bytes 3538952 | tf_op jit(solution)/shard_map/ppermute | solution.py:13
  114.3 216.2 %reduce-scatter.2.cloned.1.call-start = ((), (), s32[]{:S(2)}) async-start(), calls=%async_computation.1 | async-start | bytes 983040 | tf_op jit(solution)/shard_map/reduce_scatter | solution.py:133
  141.0 1.2 copy-start.3
  146.2 1.2 copy-start.3
  151.4 1.2 copy-start.3
  156.6 1.2 copy-start.3
  161.8 1.2 copy-start.3
  167.0 1.2 copy-start.3
  171.3 38.6 %copy-start.9 = (f32[64]{0:T(128)S(1)}, f32[64]{0:T(128)}, u32[]{:S(2)}) copy-start(f32[64]{0:T(128)} %param.17) | copy-start | bytes 772
  171.3 10.0 %collective-permute-start.4 = (bf16[1,2,2,2,1,192,1,128]{7,5,4,3,2,1,6,0:T(8,128)(2,1)S(1)}, bf16[1,2,2,2,1,192,1,128]{7,5,4,3,2,1,6,0:T(8,128)(2,1)S(1)}, u32[]{:S(2)}, u32[]{:S(2)}) collective-permute-start(bf16[1,2,2,2,1,192,1,128]{7,5,4,3,2,1,6,0:T(8,128)(2,1)S(1)} %constant_dynamic-slice_fusion.3), channel_id=1, source_target_pairs={{0,4},{4,0},{8,12},{12,8},{16,20},{20,16},{24,28},{28,24},{32,36},... | collective-permute-start | bytes 1179656 | tf_op jit(solution)/shard_map/ppermute | solution.py:13
  183.2 8.9 %collective-permute-start.5 = (bf16[1,2,2,1,2,192,1,128]{7,5,4,3,2,1,6,0:T(8,128)(2,1)S(1)}, bf16[1,2,2,1,2,192,1,128]{7,5,4,3,2,1,6,0:T(8,128)(2,1)S(1)}, u32[]{:S(2)}, u32[]{:S(2)}) collective-permute-start(bf16[1,2,2,1,2,192,1,128]{7,5,4,3,2,1,6,0:T(8,128)(2,1)S(1)} %constant_dynamic-slice_fusion.2), channel_id=1, source_target_pairs={{0,8},{4,12},{8,0},{12,4},{16,24},{20,28},{24,16},{28,20},{32,40},... | collective-permute-start | bytes 1179656 | tf_op jit(solution)/shard_map/ppermute | solution.py:13
  193.9 10.0 %collective-permute-start.6 = (bf16[1,2,1,2,2,192,1,128]{7,5,4,3,2,1,6,0:T(8,128)(2,1)S(1)}, bf16[1,2,1,2,2,192,1,128]{7,5,4,3,2,1,6,0:T(8,128)(2,1)S(1)}, u32[]{:S(2)}, u32[]{:S(2)}) collective-permute-start(bf16[1,2,1,2,2,192,1,128]{7,5,4,3,2,1,6,0:T(8,128)(2,1)S(1)} %constant_dynamic-slice_fusion.1), channel_id=1, source_target_pairs={{0,16},{4,20},{8,24},{12,28},{16,0},{20,4},{24,8},{28,12},{32,48},... | collective-permute-start | bytes 1179656 | tf_op jit(solution)/shard_map/ppermute | solution.py:13
  205.8 9.1 %collective-permute-start.7 = (bf16[1,1,2,2,2,192,1,128]{7,5,4,3,2,1,6,0:T(8,128)(2,1)S(1)}, bf16[1,1,2,2,2,192,1,128]{7,5,4,3,2,1,6,0:T(8,128)(2,1)S(1)}, u32[]{:S(2)}, u32[]{:S(2)}) collective-permute-start(bf16[1,1,2,2,2,192,1,128]{7,5,4,3,2,1,6,0:T(8,128)(2,1)S(1)} %constant_dynamic-slice_fusion), channel_id=1, source_target_pairs={{0,32},{4,36},{8,40},{12,44},{16,48},{20,52},{24,56},{28,60},{32,0... | collective-permute-start | bytes 1179656 | tf_op jit(solution)/shard_map/ppermute | solution.py:13
  217.7 2.0 copy-start.7
  219.6 179.8 %all-gather.5.cloned.1.call-start = ((), (), s32[]{:S(2)}) async-start(), calls=%async_computation.3 | async-start | bytes 5898240 | tf_op jit(solution)/shard_map/all_gather | solution.py:151
  330.4 3.3 copy-start
  330.4 3.3 copy-start.4
  333.7 1.2 copy-start.2
  336.4 69.2 %copy-start.8 = (f32[3072]{0:T(1024)S(1)}, f32[3072]{0:T(1024)}, u32[]{:S(2)}) copy-start(f32[3072]{0:T(1024)} %param.20) | copy-start | bytes 36868
  411.9 10.3 %copy-start.1 = (f32[192,3072]{1,0:T(8,128)S(1)}, f32[192,3072]{1,0:T(8,128)}, u32[]{:S(2)}) copy-start(f32[192,3072]{1,0:T(8,128)} %get-tuple-element.56) | copy-start | bytes 7077892
Sparse Core Ops, SparseCore 0:
  114.4 215.9 all-gather.2
Sparse Core Ops, SparseCore 1:
  219.7 39.8 reduce-scatter.1
  336.5 62.8 all-gather.4
